TPU v7x, 32 devices: a whole 2x2x4 slice. The times are simulated.
32 devices in a mesh: rep: 4 (over y, x), fsdp: 2 (over core), tp: 4 (over z).
Axes of the slice: x: 2, y: 2, z: 4, core: 2. Of those that a mesh axis runs over, the one named last changes fastest.
Arguments:
- grad_parts: bfloat16 [2, 2, 8192, 1024], P('fsdp', None, 'rep', 'tp'), may hold values from -4 to 4
- master_weight: float32 [2, 8192, 1024], P(None, ('rep', 'fsdp'), 'tp'), may hold values from -0.0625 to 0.0625
- moment_one: float32 [2, 8192, 1024], P(None, ('rep', 'fsdp'), 'tp'), may hold values from -4 to 4
- moment_two: float32 [2, 8192, 1024], P(None, ('rep', 'fsdp'), 'tp'), may hold values from 0.1 to 2
- layer_inputs: bfloat16 [384, 4, 8192], P(('rep', 'fsdp'), None, 'tp'), may hold values from -6 to 6
- queries: bfloat16 [384, 4, 8192], P(('rep', 'fsdp'), None, 'tp'), may hold values from -105 to 105
- kv_cache: bfloat16 [384, 24, 2, 1024], P(('rep', 'fsdp'), None, None, 'tp'), may hold values from -4 to 4
- lengths: int32 [384], P(('rep', 'fsdp')), may hold values from 2 to 24
Outputs:
- new_master: float32 [2, 8192, 1024], P(None, ('rep', 'fsdp'), 'tp')
- new_moment_one: float32 [2, 8192, 1024], P(None, ('rep', 'fsdp'), 'tp')
- new_moment_two: float32 [2, 8192, 1024], P(None, ('rep', 'fsdp'), 'tp')
- context: bfloat16 [384, 4, 8192], P(('rep', 'fsdp'), None, 'tp')
Inputs may be any that keep to these rules, and one draw needn't show every extreme that they name: lengths[r] is the number of valid cached positions of row r, at most 24.
All inputs are finite; a program needn't handle non-finite values.
Results may differ from a plain program's by a relative error of at most 0.0065.
Values may be sent and summed in bfloat16 or wider, within the bound.
A program may use at most 64 MiB of HBM per device.

v0:
```python
import jax
import jax.numpy as jnp
from jax import lax
from jax.sharding import PartitionSpec as P

HD = 128
beta_one = 0.9
beta_two = 0.95
learning_rate = 0.001
weight_decay = 0.1
epsilon = 1e-08
first_bias = 1.0 - 0.9**10
second_bias = 1.0 - 0.95**10


def adamw_update(gradient, master, moment_one, moment_two):
    new_one = beta_one * moment_one + (1.0 - beta_one) * gradient
    new_two = beta_two * moment_two + (1.0 - beta_two) * gradient * gradient
    update = new_one / first_bias / (jnp.sqrt(new_two / second_bias) + epsilon)
    new_master = master - learning_rate * (update + weight_decay * master)
    return (new_one, new_two, new_master)


def attend(queries, kv_cache, fresh_keys, fresh_values, lengths):
    row_count = queries.shape[0]
    step_count = queries.shape[1]
    kv_heads = fresh_keys.shape[2]
    cache_len = kv_cache.shape[1]
    grouped = queries.reshape(row_count, step_count, kv_heads, -1, HD)
    cached_keys = kv_cache[:, :, 0].reshape(row_count, cache_len, kv_heads, HD)
    cached_values = kv_cache[:, :, 1].reshape(row_count, cache_len, kv_heads, HD)
    scaling = 1.0 / jnp.sqrt(jnp.float32(HD))
    cached_scores = (
        jnp.einsum("rsgqd,rcgd->rsgqc", grouped, cached_keys, preferred_element_type=jnp.float32)
        * scaling
    )
    fresh_scores = (
        jnp.einsum("rsgqd,rugd->rsgqu", grouped, fresh_keys, preferred_element_type=jnp.float32)
        * scaling
    )
    valid_old = jnp.arange(cache_len, dtype=jnp.int32)[None, :] < lengths[:, None]
    valid_old = valid_old[:, None, None, None, :]
    steps_index = jnp.arange(step_count, dtype=jnp.int32)
    valid_new = (steps_index[None, :] <= steps_index[:, None])[None, :, None, None, :]
    scores = jnp.concatenate(
        [
            jnp.where(valid_old, cached_scores, -jnp.inf),
            jnp.where(valid_new, fresh_scores, -jnp.inf),
        ],
        axis=-1,
    )
    row_max = jnp.max(scores, axis=-1, keepdims=True)
    exponent = jnp.exp(scores - row_max)
    weights = (exponent / jnp.sum(exponent, axis=-1, keepdims=True)).astype(jnp.bfloat16)
    output = jnp.einsum(
        "rsgqc,rcgd->rsgqd",
        weights[..., :cache_len],
        cached_values,
        preferred_element_type=jnp.float32,
    )
    output = output + jnp.einsum(
        "rsgqu,rugd->rsgqd",
        weights[..., cache_len:],
        fresh_values,
        preferred_element_type=jnp.float32,
    )
    return output.astype(jnp.bfloat16).reshape(row_count, step_count, -1)


def on_device(
    grad_parts, master_weight, moment_one, moment_two, layer_inputs, queries, kv_cache, lengths
):
    gradient = lax.psum_scatter(
        grad_parts[0].astype(jnp.float32).astype(jnp.bfloat16),
        "fsdp",
        scatter_dimension=1,
        tiled=True,
    ).astype(jnp.float32)
    new_one, new_two, new_master = adamw_update(gradient, master_weight, moment_one, moment_two)
    rollout_weight = new_master.astype(jnp.bfloat16)
    row_count = layer_inputs.shape[0]
    step_count = layer_inputs.shape[1]
    gathered = lax.all_gather(layer_inputs, "tp", axis=2, tiled=True)
    flattened = gathered.reshape(row_count * step_count, gathered.shape[2])
    projected = jnp.einsum(
        "td,kdc->ktc",
        flattened,
        lax.all_gather(rollout_weight, ("rep", "fsdp"), axis=1, tiled=True),
        preferred_element_type=jnp.float32,
    )
    fresh_pair = projected.astype(jnp.bfloat16).reshape(2, row_count, step_count, -1, HD)
    context = attend(queries, kv_cache, fresh_pair[0], fresh_pair[1], lengths)
    return (new_master, new_one, new_two, context)


def solution(mesh):
    return jax.shard_map(
        on_device,
        mesh=mesh,
        in_specs=(
            P("fsdp", None, "rep", "tp"),
            P(None, ("rep", "fsdp"), "tp"),
            P(None, ("rep", "fsdp"), "tp"),
            P(None, ("rep", "fsdp"), "tp"),
            P(("rep", "fsdp"), None, "tp"),
            P(("rep", "fsdp"), None, "tp"),
            P(("rep", "fsdp"), None, None, "tp"),
            P(("rep", "fsdp")),
        ),
        out_specs=(
            P(None, ("rep", "fsdp"), "tp"),
            P(None, ("rep", "fsdp"), "tp"),
            P(None, ("rep", "fsdp"), "tp"),
            P(("rep", "fsdp"), None, "tp"),
        ),
        check_vma=False,
    )
```

profile of v0, /device:TPU:0, one launch (start us, length us, event | category | flops | bytes accessed | tf_op | source)
XLA Modules:
  0.0 160.2 jit_solution(18076196282730567113)
XLA Ops:
  8.1 0.7 reduce-scatter.2.cloned.1.call-update
  8.8 0.5 all-gather.5.cloned.1.call-update
  9.4 14.2 %reduce-scatter.2.cloned.1.call-done = bf16[2,1024,256]{2,1,0:T(8,128)(2,1)} async-done(((bf16[2,2048,256]{2,1,0:T(8,128)(2,1)}), bf16[2,1024,256]{2,1,0:T(8,128)(2,1)}) %reduce-scatter.2.cloned.1.call-update) | async-done | bytes 1048592 | tf_op jit(solution)/shard_map/reduce_scatter | solution.py:73
  23.6 6.7 %fusion.17 = (bf16[2,1024,256]{2,1,0:T(8,128)(2,1)}, f32[2,1024,256]{2,1,0:T(8,128)}, f32[2,1024,256]{2,1,0:T(8,128)}, f32[2,1024,256]{2,1,0:T(8,128)}) fusion(f32[2,1024,256]{2,1,0:T(8,128)S(1)} %copy-done.2, bf16[2,1024,256]{2,1,0:T(8,128)(2,1)} %reduce-scatter.2.cloned.1.call-done, f32[2,1024,256]{2,1,0:T(8,128)} %param.10, f32[2,1024,256]{2,1,0:T(8,128)} %param.11), kind=kLoop, calls=%fused_computation.30 | loop fusion | flops 8912896 | bytes 14680064 | tf_op jit(solution)/shard_map/convert_element_type | solution.py:80
  30.3 0.5 reshape.57
  30.8 0.7 copy-done.1
  31.5 4.9 %slice_reduce_fusion = (bf16[48,24,256]{2,1,0:T(8,128)(2,1)S(1)}, bf16[48,24,256]{2,1,0:T(8,128)(2,1)S(1)}) fusion(bf16[48,24,2,256]{3,2,1,0:T(2,128)(2,1)S(1)} %copy-done.1), kind=kLoop, calls=%fused_computation.11 | loop fusion | bytes 2359296 | tf_op jit(solution)/shard_map/slice | solution.py:31
  36.4 1.0 reshape_squeeze.6
  37.4 1.0 reshape_squeeze.7
  38.4 1.7 %fusion.21 = (f32[48,4,2,8]{3,1,2,0:T(4,128)S(1)}, f32[48,4,2,8,24]{4,3,1,2,0:T(8,128)S(1)}) fusion(bf16[48,4,2,8,128]{4,3,2,1,0:T(8,128)(2,1)S(1)} %reshape.57, bf16[48,24,2,128,1]{3,2,1,0,4:T(2,128)(2,1)} %bitcast.23, pred[48,24]{1,0:T(8,128)(4,1)S(1)} %iota_compare_fusion), kind=kOutput, calls=%fused_computation.32 | convolution fusion | flops 19092480 | bytes 1684608 | tf_op jit(solution)/shard_map/rsgqd,rcgd->rsgqc/dot_general | solution.py:34
  40.1 36.7 %all-gather.5.cloned.1.call-done = bf16[48,4,8192]{2,1,0:T(4,128)(2,1)} async-done(((bf16[48,4,2048]{2,1,0:T(4,128)(2,1)}), bf16[48,4,8192]{2,1,0:T(4,128)(2,1)}) %all-gather.5.cloned.1.call-update) | async-done | bytes 3145744 | tf_op jit(solution)/shard_map/all_gather | solution.py:83
  76.9 5.5 %reshape.61 = bf16[192,8192,1]{1,0,2:T(8,128)(2,1)} reshape(bf16[48,4,8192]{2,1,0:T(4,128)(2,1)} %all-gather.5.cloned.1.call-done) | data formatting | bytes 6291456 | tf_op jit(solution)/shard_map/reshape | solution.py:84
  82.3 49.1 %all-gather.3.cloned.1.call-done = bf16[2,8192,256]{2,1,0:T(8,128)(2,1)} async-done(((bf16[2,1024,256]{2,1,0:T(8,128)(2,1)}), bf16[2,8192,256]{2,1,0:T(8,128)(2,1)}) %all-gather.3.cloned.1.call-update) | async-done | bytes 8388624 | tf_op jit(solution)/shard_map/all_gather | solution.py:88
  131.4 6.1 %fusion.4 = bf16[2,192,256]{2,1,0:T(8,128)(2,1)S(1)} fusion(bf16[192,8192,1]{1,0,2:T(8,128)(2,1)} %reshape.61, bf16[2,8192,256]{2,1,0:T(8,128)(2,1)} %all-gather.3.cloned.1.call-done), kind=kOutput, calls=%fused_computation.14 | convolution fusion | flops 1610711040 | bytes 11730944 | tf_op jit(solution)/shard_map/td,kdc->ktc/dot_general | solution.py:85
  137.6 0.6 fusion.20
  138.2 3.5 %fusion.8 = f32[48,2,4,4,8]{4,2,3,1,0:T(4,128)S(1)} fusion(bf16[48,4,2,8,128]{4,3,2,1,0:T(8,128)(2,1)S(1)} %reshape.57, bf16[48,4,2,128,1]{3,2,1,0,4:T(2,128)(2,1)S(1)} %bitcast.26), kind=kOutput, calls=%fused_computation.18 | convolution fusion | flops 3145728 | bytes 933888 | tf_op jit(solution)/shard_map/rsgqd,rugd->rsgqu/dot_general | solution.py:38
  141.8 0.5 copy.55
  142.3 0.7 fusion.16
  143.2 2.4 %copy.56 = f32[48,4,2,8,4]{4,3,1,2,0:T(8,128)S(1)} copy(f32[48,4,2,8,4]{0,3,1,4,2:T(8,128)} %get-tuple-element.23) | data formatting | bytes 98304 | tf_op jit(solution)/shard_map/jit(_where)/select_n | solution.py:48
  145.6 1.5 fusion.13
  147.1 2.2 %divide_convert_fusion = bf16[48,4,2,8,28]{4,3,1,2,0:T(8,128)(2,1)} fusion(f32[48,4,2,8]{3,1,2,0:T(4,128)S(1)} %fusion.13, f32[48,4,2,8]{3,1,2,0:T(4,128)S(1)} %reduce_max.22, f32[48,4,2,8,4]{4,3,1,2,0:T(8,128)S(1)} %copy.56, f32[48,4,2,8,24]{4,3,1,2,0:T(8,128)S(1)} %get-tuple-element.31), kind=kLoop, calls=%fused_computation.9 | loop fusion | flops 344064 | bytes 540672 | tf_op jit(solution)/shard_map/convert_element_type | solution.py:54
  149.3 1.7 %fusion.6 = f32[48,2,4,8,128]{4,3,2,1,0:T(8,128)S(1)} fusion(bf16[48,4,2,8,28]{4,3,1,2,0:T(8,128)(2,1)} %divide_convert_fusion, bf16[48,24,2,128,1]{3,2,1,0,4:T(2,128)(2,1)} %bitcast.22), kind=kOutput, calls=%fused_computation.16 | convolution fusion | flops 18874368 | bytes 2334720 | tf_op jit(solution)/shard_map/rsgqc,rcgd->rsgqd/dot_general | solution.py:55
  151.1 0.4 fusion.3
  151.7 1.1 reshape.66
  (22 shorter events, 0.6 us)
Async XLA Ops:
  8.0 15.6 %copy-start.2 = (f32[2,1024,256]{2,1,0:T(8,128)S(1)}, f32[2,1024,256]{2,1,0:T(8,128)}, u32[]{:S(2)}) copy-start(f32[2,1024,256]{2,1,0:T(8,128)} %param.9) | copy-start | bytes 6291460
  8.0 15.6 %reduce-scatter.2.cloned.1.call-start = ((), (), s32[]{:S(2)}) async-start(), calls=%async_computation.1 | async-start | bytes 3145728 | tf_op jit(solution)/shard_map/reduce_scatter | solution.py:73
  8.7 68.1 %all-gather.5.cloned.1.call-start = ((), (), s32[]{:S(2)}) async-start(), calls=%async_computation.3 | async-start | bytes 3932160 | tf_op jit(solution)/shard_map/all_gather | solution.py:83
  9.3 20.9 %copy-start.3 = (bf16[48,4,2048]{2,1,0:T(4,128)(2,1)S(1)}, bf16[48,4,2048]{2,1,0:T(4,128)(2,1)}, u32[]{:S(2)}) copy-start(bf16[48,4,2048]{2,1,0:T(4,128)(2,1)} %param.13) | copy-start | bytes 2359300
  9.3 122.1 %all-gather.3.cloned.1.call-start = ((), (), s32[]{:S(2)}) async-start(), calls=%async_computation.2 | async-start | bytes 9437184 | tf_op jit(solution)/shard_map/all_gather | solution.py:88
  30.2 1.3 copy-start.1
  31.5 6.8 %copy-start.5 = (s32[48]{0:T(128)S(1)}, s32[48]{0:T(128)}, u32[]{:S(2)}) copy-start(s32[48]{0:T(128)} %param.15) | copy-start | bytes 580
  147.1 2.2 %copy-start.4 = (bf16[1,192,256]{2,1,0:T(8,128)(2,1)S(1)}, bf16[1,192,256]{2,1,0:T(8,128)(2,1)}, u32[]{:S(2)}) copy-start(bf16[1,192,256]{2,1,0:T(8,128)(2,1)} %get-tuple-element.28) | copy-start | bytes 294916
  149.3 1.8 %copy-start = (bf16[48,4,2,8,28]{4,3,1,2,0:T(8,128)(2,1)S(1)}, bf16[48,4,2,8,28]{4,3,1,2,0:T(8,128)(2,1)}, u32[]{:S(2)}) copy-start(bf16[48,4,2,8,28]{4,3,1,2,0:T(8,128)(2,1)} %divide_convert_fusion) | copy-start | bytes 516100
Sparse Core Ops, SparseCore 0:
  11.1 12.4 reduce-scatter.1
Sparse Core Ops, SparseCore 1:
  10.8 66.0 all-gather.4
  78.6 52.8 all-gather.2
where the time goes:
time: 161 us; the launch traced here: 160 us
  waiting for transfers between devices  101 us (63%)
  local copies, waits for them, and re-layouts  18.4 us (11%)
  between operations  15.6 us (10%)
  matrix products  13.6 us (8%)
  other arithmetic  11.2 us (7%)
    all_gather x1, waiting for transfers between devices, on_device(): lax.all_gather(rollout_weight, ('rep', 'fsdp'), axis=1, tiled=True)  49.1 us
    all_gather x1, waiting for transfers between devices, on_device(): gathered = lax.all_gather(layer_inputs, 'tp', axis=2, tiled=True)  36.7 us
    reduce_scatter x1, waiting for transfers between devices, on_device(): lax.psum_scatter(grad_parts[0].astype(jnp.float32).astype(jnp.bfloat16),...  14.2 us
    convert_element_type x1, other arithmetic, on_device(): rollout_weight = new_master.astype(jnp.bfloat16)  6.66 us
    dot_general x1, matrix products, on_device(): jnp.einsum('td,kdc->ktc', flattened, lax.all_gather(rollout_weight, ('rep...  6.13 us
    reshape x1, local copies, waits for them, and re-layouts, on_device(): flattened = gathered.reshape(row_count * step_count, gathered.shape[2])  5.49 us
    slice x1, local copies, waits for them, and re-layouts, attend(): kv_cache[:, :, 1].reshape(row_count, cache_len, kv_heads, HD)  4.9 us
    dot_general x1, matrix products, attend(): jnp.einsum('rsgqd,rugd->rsgqu', grouped, fresh_keys, preferred_element_ty...  3.54 us
  transfers between devices with their start and end apart: 3, of which 3 were waited for; matrix products, arithmetic and copies ran while one was open for 13% of the time, Pallas kernels for 0%

commit v1 on v0

--- a/solution.py
+++ b/solution.py
@@ -1,3 +1,4 @@
+import functools
 import jax
 import jax.numpy as jnp
 from jax import lax
@@ -11,6 +12,22 @@
 epsilon = 1e-08
 first_bias = 1.0 - 0.9**10
 second_bias = 1.0 - 0.95**10
+
+
+def shape_case(content, mesh_ax, dimension_no):
+    n_chips = lax.axis_size(mesh_ax)
+    rows = list(map(lambda no: (no, (no + 1) % n_chips), range(n_chips)))
+    step_out = [None] * n_chips
+    step_out[n_chips - 1] = content
+    for ii in range(n_chips - 2, -1, -1):
+        step_out[ii] = lax.ppermute(step_out[ii + 1], mesh_ax, rows)
+    front = jnp.concatenate(step_out, axis=dimension_no)
+    frame_out = (lax.axis_index(mesh_ax) + 1) * content.shape[dimension_no]
+    back = jnp.roll(front, frame_out, dimension_no)
+    return back
+
+
+digits_link = functools.partial(shape_case, mesh_ax="tp", dimension_no=2)
 
 
 def adamw_update(gradient, master, moment_one, moment_two):
@@ -80,7 +97,7 @@
     rollout_weight = new_master.astype(jnp.bfloat16)
     row_count = layer_inputs.shape[0]
     step_count = layer_inputs.shape[1]
-    gathered = lax.all_gather(layer_inputs, "tp", axis=2, tiled=True)
+    gathered = digits_link(layer_inputs)
     flattened = gathered.reshape(row_count * step_count, gathered.shape[2])
     projected = jnp.einsum(
         "td,kdc->ktc",

time: 161 us -> 139 us (0.86)
  waiting for transfers between devices: 101 us -> 63.1 us
  local copies, waits for them, and re-layouts: 18.4 us -> 33.3 us
  starting transfers between devices: 0.12 us -> 1.98 us
    all_gather x1, waiting for transfers between devices: 49.1 us -> 0.01 us  [on_device(): lax.all_gather(rollout_weight, ('rep', 'fsdp'), axis=1, tiled=True)]
    ppermute x0 -> x3, waiting for transfers between devices: none -> 47.6 us  [shape_case(): step_out[ii] = lax.ppermute(step_out[ii + 1], mesh_ax, rows)]
    all_gather x1 -> x0, waiting for transfers between devices: 36.7 us -> none  [on_device(): gathered = lax.all_gather(layer_inputs, 'tp', axis=2, tiled=True)]
    unnamed x14 -> x25, local copies, waits for them, and re-layouts: 1.95 us -> 8.69 us
    dynamic_slice x0 -> x1, local copies, waits for them, and re-layouts: none -> 3.07 us  [shape_case(): back = jnp.roll(front, frame_out, dimension_no)]
    ppermute x0 -> x3, starting transfers between devices: none -> 1.91 us  [shape_case(): step_out[ii] = lax.ppermute(step_out[ii + 1], mesh_ax, rows)]
  transfers between devices with their start and end apart: 3 -> 5, of which waited for: 3 -> 4; matrix products, arithmetic and copies ran while one was open for 13% -> 21% of each run, Pallas kernels for 0% -> 0%
where the time goes in v1:
time: 139 us
  waiting for transfers between devices  63.1 us (45%)
  local copies, waits for them, and re-layouts  33.3 us (24%)
  between operations  14.2 us (10%)
  matrix products  13.6 us (10%)
  other arithmetic  12.6 us (9%)
  starting transfers between devices  1.98 us (1%)
    ppermute x3, waiting for transfers between devices, shape_case(): step_out[ii] = lax.ppermute(step_out[ii + 1], mesh_ax, rows)  47.6 us
    reduce_scatter x1, waiting for transfers between devices, on_device(): lax.psum_scatter(grad_parts[0].astype(jnp.float32).astype(jnp.bfloat16),...  14.8 us
    unnamed x25, local copies, waits for them, and re-layouts  8.69 us
    convert_element_type x1, other arithmetic, on_device(): rollout_weight = new_master.astype(jnp.bfloat16)  7.37 us
    dot_general x1, matrix products, on_device(): jnp.einsum('td,kdc->ktc', flattened, lax.all_gather(rollout_weight, ('rep...  6.13 us
    slice x1, local copies, waits for them, and re-layouts, attend(): kv_cache[:, :, 1].reshape(row_count, cache_len, kv_heads, HD)  5.88 us
    reshape x1, local copies, waits for them, and re-layouts, on_device(): flattened = gathered.reshape(row_count * step_count, gathered.shape[2])  5.48 us
    dot_general x1, matrix products, attend(): jnp.einsum('rsgqd,rugd->rsgqu', grouped, fresh_keys, preferred_element_ty...  3.54 us
  transfers between devices with their start and end apart: 5, of which 4 were waited for; matrix products, arithmetic and copies ran while one was open for 21% of the time, Pallas kernels for 0%

profile of v1, /device:TPU:0, one launch (start us, length us, event | category | flops | bytes accessed | tf_op | source)
XLA Modules:
  0.0 138.8 jit_solution(11561586046683696303)
XLA Ops:
  8.0 14.8 %reduce-scatter.2.cloned.1.call-done = bf16[2,1024,256]{2,1,0:T(8,128)(2,1)} async-done(((bf16[2,2048,256]{2,1,0:T(8,128)(2,1)}), bf16[2,1024,256]{2,1,0:T(8,128)(2,1)}) %reduce-scatter.2.cloned.1.call-update) | async-done | bytes 1048592 | tf_op jit(solution)/shard_map/reduce_scatter | solution.py:90
  22.7 7.4 %fusion.17 = (bf16[2,1024,256]{2,1,0:T(8,128)(2,1)}, f32[2,1024,256]{2,1,0:T(8,128)}, f32[2,1024,256]{2,1,0:T(8,128)}, f32[2,1024,256]{2,1,0:T(8,128)}) fusion(f32[2,1024,256]{2,1,0:T(8,128)} %param.9, bf16[2,1024,256]{2,1,0:T(8,128)(2,1)} %reduce-scatter.2.cloned.1.call-done, f32[2,1024,256]{2,1,0:T(8,128)} %param.10, f32[2,1024,256]{2,1,0:T(8,128)} %param.11), kind=kLoop, calls=%fused_computation.39 | loop fusion | flops 8912896 | bytes 14680064 | tf_op jit(solution)/shard_map/convert_element_type | solution.py:97
  30.1 1.9 %collective-permute-start = (bf16[48,4,2048]{2,1,0:T(4,128)(2,1)S(1)}, bf16[48,4,2048]{2,1,0:T(4,128)(2,1)S(1)}, u32[]{:S(2)}, u32[]{:S(2)}) collective-permute-start(bf16[48,4,2048]{2,1,0:T(4,128)(2,1)S(1)} %copy-done.2), channel_id=1, source_target_pairs={{0,1},{1,2},{2,3},{3,0},{4,5},{5,6},{6,7},{7,4},{8,9},{9,10},{10,1... | collective-permute-start | bytes 2359304 | tf_op jit(solution)/shard_map/ppermute | solution.py:23
  32.0 19.7 %collective-permute-done = bf16[48,4,2048]{2,1,0:T(4,128)(2,1)S(1)} collective-permute-done((bf16[48,4,2048]{2,1,0:T(4,128)(2,1)S(1)}, bf16[48,4,2048]{2,1,0:T(4,128)(2,1)S(1)}, u32[]{:S(2)}, u32[]{:S(2)}) %collective-permute-start) | collective-permute-done | bytes 786464 | tf_op jit(solution)/shard_map/ppermute | solution.py:23
  51.8 20.8 %collective-permute-done.1 = bf16[48,4,2048]{2,1,0:T(4,128)(2,1)} collective-permute-done((bf16[48,4,2048]{2,1,0:T(4,128)(2,1)S(1)}, bf16[48,4,2048]{2,1,0:T(4,128)(2,1)}, u32[]{:S(2)}, u32[]{:S(2)}) %collective-permute-start.1) | collective-permute-done | bytes 786464 | tf_op jit(solution)/shard_map/ppermute | solution.py:23
  72.6 5.9 %slice_reduce_fusion = (bf16[48,24,256]{2,1,0:T(8,128)(2,1)}, bf16[48,24,256]{2,1,0:T(8,128)(2,1)}) fusion(bf16[48,24,2,256]{3,2,1,0:T(2,128)(2,1)S(1)} %copy-done.1), kind=kLoop, calls=%fused_computation.11 | loop fusion | bytes 2359296 | tf_op jit(solution)/shard_map/slice | solution.py:48
  78.5 1.9 %reshape.57 = bf16[48,4,2,8,128]{4,3,2,1,0:T(8,128)(2,1)S(1)} reshape(bf16[48,4,2048]{2,1,0:T(4,128)(2,1)} %param.13) | data formatting | bytes 1572864 | tf_op jit(solution)/shard_map/reshape | solution.py:46
  80.4 2.5 %reshape_squeeze.6 = bf16[48,24,2,128]{3,2,1,0:T(2,128)(2,1)} reshape(bf16[48,24,256]{2,1,0:T(8,128)(2,1)} %get-tuple-element.21) | data formatting | bytes 1179648 | tf_op jit(solution)/shard_map/reshape;squeeze | solution.py:47
  83.9 1.7 %fusion.21 = (f32[48,4,2,8]{3,1,2,0:T(4,128)S(1)}, f32[48,4,2,8,24]{4,3,1,2,0:T(8,128)S(1)}) fusion(bf16[48,4,2,8,128]{4,3,2,1,0:T(8,128)(2,1)S(1)} %reshape.57, bf16[48,24,2,128,1]{3,2,1,0,4:T(2,128)(2,1)} %bitcast.23, pred[48,24]{1,0:T(8,128)(4,1)S(1)} %iota_compare_fusion), kind=kOutput, calls=%fused_computation.41 | convolution fusion | flops 19092480 | bytes 1684608 | tf_op jit(solution)/shard_map/rsgqd,rcgd->rsgqc/dot_general | solution.py:51
  85.6 7.1 %collective-permute-done.2 = bf16[48,4,2048]{2,1,0:T(4,128)(2,1)} collective-permute-done((bf16[48,4,2048]{2,1,0:T(4,128)(2,1)}, bf16[48,4,2048]{2,1,0:T(4,128)(2,1)}, u32[]{:S(2)}, u32[]{:S(2)}) %collective-permute-start.2) | collective-permute-done | bytes 786464 | tf_op jit(solution)/shard_map/ppermute | solution.py:23
  92.7 1.5 %constant_dynamic-update-slice_fusion.7 = bf16[48,4,16384]{2,1,0:T(4,128)(2,1)S(1)} fusion(bf16[48,4,2048]{2,1,0:T(4,128)(2,1)} %collective-permute-done.2), kind=kLoop, calls=%fused_computation.35 | loop fusion | bytes 1572864
  94.2 1.6 %constant_dynamic-update-slice_fusion.6 = bf16[48,4,16384]{2,1,0:T(4,128)(2,1)S(1)} fusion(bf16[48,4,16384]{2,1,0:T(4,128)(2,1)S(1)} %constant_dynamic-update-slice_fusion.7, bf16[48,4,2048]{2,1,0:T(4,128)(2,1)} %collective-permute-done.1), kind=kLoop, calls=%fused_computation.34 | loop fusion | bytes 1572864
  96.7 1.6 %constant_dynamic-update-slice_fusion.3 = bf16[48,4,16384]{2,1,0:T(4,128)(2,1)S(1)} fusion(bf16[48,4,16384]{2,1,0:T(4,128)(2,1)S(1)} %constant_dynamic-update-slice_fusion.4, bf16[48,4,2048]{2,1,0:T(4,128)(2,1)} %collective-permute-done.2), kind=kLoop, calls=%fused_computation.31 | loop fusion | bytes 1572864
  98.3 1.6 %constant_dynamic-update-slice_fusion.2 = bf16[48,4,16384]{2,1,0:T(4,128)(2,1)S(1)} fusion(bf16[48,4,16384]{2,1,0:T(4,128)(2,1)S(1)} %constant_dynamic-update-slice_fusion.3, bf16[48,4,2048]{2,1,0:T(4,128)(2,1)} %collective-permute-done.1), kind=kLoop, calls=%fused_computation.30 | loop fusion | bytes 1572864
  100.7 3.1 %constant_dynamic-slice_fusion = bf16[48,4,8192]{2,1,0:T(4,128)(2,1)} fusion(bf16[48,4,16384]{2,1,0:T(4,128)(2,1)S(1)} %constant_dynamic-update-slice_fusion, s32[]{:T(128)S(6)} %select_n.27), kind=kLoop, calls=%fused_computation.37 | loop fusion | bytes 6291460 | tf_op jit(solution)/shard_map/jit(_roll_dynamic)/dynamic_slice | solution.py:26
  103.8 5.5 %reshape.61 = bf16[192,8192,1]{1,0,2:T(8,128)(2,1)} reshape(bf16[48,4,8192]{2,1,0:T(4,128)(2,1)} %constant_dynamic-slice_fusion) | data formatting | bytes 6291456 | tf_op jit(solution)/shard_map/reshape | solution.py:101
  109.3 6.1 %fusion.4 = bf16[2,192,256]{2,1,0:T(8,128)(2,1)S(1)} fusion(bf16[192,8192,1]{1,0,2:T(8,128)(2,1)} %reshape.61, bf16[2,8192,256]{2,1,0:T(8,128)(2,1)} %all-gather.2.cloned.1.call-done), kind=kOutput, calls=%fused_computation.14 | convolution fusion | flops 1610711040 | bytes 11730944 | tf_op jit(solution)/shard_map/td,kdc->ktc/dot_general | solution.py:102
  116.1 3.5 %fusion.8 = f32[48,2,4,4,8]{4,2,3,1,0:T(4,128)S(1)} fusion(bf16[48,4,2,8,128]{4,3,2,1,0:T(8,128)(2,1)S(1)} %reshape.57, bf16[48,4,2,128,1]{3,2,1,0,4:T(2,128)(2,1)S(1)} %bitcast.26), kind=kOutput, calls=%fused_computation.18 | convolution fusion | flops 3145728 | bytes 933888 | tf_op jit(solution)/shard_map/rsgqd,rugd->rsgqu/dot_general | solution.py:55
  120.1 1.4 fusion.16
  121.5 2.4 %copy.56 = f32[48,4,2,8,4]{4,3,1,2,0:T(8,128)S(1)} copy(f32[48,4,2,8,4]{0,3,1,4,2:T(8,128)} %get-tuple-element.23) | data formatting | bytes 98304 | tf_op jit(solution)/shard_map/jit(_where)/select_n | solution.py:65
  124.8 1.5 %fusion.13 = f32[48,4,2,8]{3,1,2,0:T(4,128)S(1)} fusion(f32[48,4,2,8]{3,1,2,0:T(4,128)S(1)} %reduce_max.22, f32[48,4,2,8,4]{4,3,1,2,0:T(8,128)S(1)} %copy.56, f32[48,4,2,8,24]{4,3,1,2,0:T(8,128)S(1)} %get-tuple-element.31), kind=kLoop, calls=%fused_computation.23 | loop fusion | flops 254976 | bytes 368640 | tf_op jit(solution)/shard_map/reduce_sum | solution.py:71
  126.3 2.2 %divide_convert_fusion = bf16[48,4,2,8,28]{4,3,1,2,0:T(8,128)(2,1)} fusion(f32[48,4,2,8]{3,1,2,0:T(4,128)S(1)} %fusion.13, f32[48,4,2,8]{3,1,2,0:T(4,128)S(1)} %reduce_max.22, f32[48,4,2,8,4]{4,3,1,2,0:T(8,128)S(1)} %copy.56, f32[48,4,2,8,24]{4,3,1,2,0:T(8,128)S(1)} %get-tuple-element.31), kind=kLoop, calls=%fused_computation.9 | loop fusion | flops 344064 | bytes 540672 | tf_op jit(solution)/shard_map/convert_element_type | solution.py:71
  128.5 1.7 %fusion.6 = f32[48,2,4,8,128]{4,3,2,1,0:T(8,128)S(1)} fusion(bf16[48,4,2,8,28]{4,3,1,2,0:T(8,128)(2,1)} %divide_convert_fusion, bf16[48,24,2,128,1]{3,2,1,0,4:T(2,128)(2,1)} %bitcast.22), kind=kOutput, calls=%fused_computation.16 | convolution fusion | flops 18874368 | bytes 2334720 | tf_op jit(solution)/shard_map/rsgqc,rcgd->rsgqd/dot_general | solution.py:72
  130.9 1.1 reshape.66
  (38 shorter events, 6.3 us)
Async XLA Ops:
  7.2 15.6 %reduce-scatter.2.cloned.1.call-start = ((), (), s32[]{:S(2)}) async-start(), calls=%async_computation.1 | async-start | bytes 3145728 | tf_op jit(solution)/shard_map/reduce_scatter | solution.py:90
  7.9 22.2 %copy-start.2 = (bf16[48,4,2048]{2,1,0:T(4,128)(2,1)S(1)}, bf16[48,4,2048]{2,1,0:T(4,128)(2,1)}, u32[]{:S(2)}) copy-start(bf16[48,4,2048]{2,1,0:T(4,128)(2,1)} %param.12) | copy-start | bytes 2359300
  7.9 101.3 %all-gather.2.cloned.1.call-start = ((), (), s32[]{:S(2)}) async-start(), calls=%async_computation.2 | async-start | bytes 9437184 | tf_op jit(solution)/shard_map/all_gather | solution.py:105
  22.7 49.9 %copy-start.1 = (bf16[48,24,2,256]{3,2,1,0:T(2,128)(2,1)S(1)}, bf16[48,24,2,256]{3,2,1,0:T(2,128)(2,1)}, u32[]{:S(2)}) copy-start(bf16[48,24,2,256]{3,2,1,0:T(2,128)(2,1)} %param.14) | copy-start | bytes 3538948
  30.1 21.6 %collective-permute-start = (bf16[48,4,2048]{2,1,0:T(4,128)(2,1)S(1)}, bf16[48,4,2048]{2,1,0:T(4,128)(2,1)S(1)}, u32[]{:S(2)}, u32[]{:S(2)}) collective-permute-start(bf16[48,4,2048]{2,1,0:T(4,128)(2,1)S(1)} %copy-done.2), channel_id=1, source_target_pairs={{0,1},{1,2},{2,3},{3,0},{4,5},{5,6},{6,7},{7,4},{8,9},{9,10},{10,1... | collective-permute-start | bytes 2359304 | tf_op jit(solution)/shard_map/ppermute | solution.py:23
  51.8 26.7 %copy-start.3 = (bf16[48,4,2048]{2,1,0:T(4,128)(2,1)}, bf16[48,4,2048]{2,1,0:T(4,128)(2,1)S(1)}, u32[]{:S(2)}) copy-start(bf16[48,4,2048]{2,1,0:T(4,128)(2,1)S(1)} %collective-permute-done) | copy-start | bytes 2359300
  51.8 20.8 %collective-permute-start.1 = (bf16[48,4,2048]{2,1,0:T(4,128)(2,1)S(1)}, bf16[48,4,2048]{2,1,0:T(4,128)(2,1)}, u32[]{:S(2)}, u32[]{:S(2)}) collective-permute-start(bf16[48,4,2048]{2,1,0:T(4,128)(2,1)S(1)} %collective-permute-done), channel_id=1, source_target_pairs={{0,1},{1,2},{2,3},{3,0},{4,5},{5,6},{6,7},{7,4},{8,9},{9,10},{10,1... | collective-permute-start | bytes 2359304 | tf_op jit(solution)/shard_map/ppermute | solution.py:23
  72.6 20.2 %collective-permute-start.2 = (bf16[48,4,2048]{2,1,0:T(4,128)(2,1)}, bf16[48,4,2048]{2,1,0:T(4,128)(2,1)}, u32[]{:S(2)}, u32[]{:S(2)}) collective-permute-start(bf16[48,4,2048]{2,1,0:T(4,128)(2,1)} %collective-permute-done.1), channel_id=1, source_target_pairs={{0,1},{1,2},{2,3},{3,0},{4,5},{5,6},{6,7},{7,4},{8,9},{9,10},{10,1... | collective-permute-start | bytes 2359304 | tf_op jit(solution)/shard_map/ppermute | solution.py:23
  78.5 4.4 %copy-start.5 = (bf16[48,24,256]{2,1,0:T(8,128)(2,1)S(1)}, bf16[48,24,256]{2,1,0:T(8,128)(2,1)}, u32[]{:S(2)}) copy-start(bf16[48,24,256]{2,1,0:T(8,128)(2,1)} %get-tuple-element.20) | copy-start | bytes 1769476
  78.5 5.3 %copy-start.7 = (s32[48]{0:T(128)S(1)}, s32[48]{0:T(128)}, u32[]{:S(2)}) copy-start(s32[48]{0:T(128)} %param.15) | copy-start | bytes 580
  85.6 10.2 %copy-start.4 = (bf16[48,4,2048]{2,1,0:T(4,128)(2,1)S(1)}, bf16[48,4,2048]{2,1,0:T(4,128)(2,1)}, u32[]{:S(2)}) copy-start(bf16[48,4,2048]{2,1,0:T(4,128)(2,1)} %copy-done.3) | copy-start | bytes 2359300
  126.3 2.2 %copy-start.6 = (bf16[1,192,256]{2,1,0:T(8,128)(2,1)S(1)}, bf16[1,192,256]{2,1,0:T(8,128)(2,1)}, u32[]{:S(2)}) copy-start(bf16[1,192,256]{2,1,0:T(8,128)(2,1)} %get-tuple-element.28) | copy-start | bytes 294916
  128.5 1.8 %copy-start = (bf16[48,4,2,8,28]{4,3,1,2,0:T(8,128)(2,1)S(1)}, bf16[48,4,2,8,28]{4,3,1,2,0:T(8,128)(2,1)}, u32[]{:S(2)}) copy-start(bf16[48,4,2,8,28]{4,3,1,2,0:T(8,128)(2,1)} %divide_convert_fusion) | copy-start | bytes 516100
Sparse Core Ops, SparseCore 0:
  10.2 12.4 reduce-scatter.1
  30.2 55.5 all-gather.1
